TPU v7x, 32 devices: a whole 2x2x4 slice. The times are simulated.
32 devices in a mesh: tm: 4 (over y, x), space: 8 (over z, core).
Axes of the slice: x: 2, y: 2, z: 4, core: 2. Of those that a mesh axis runs over, the one named last changes fastest.
Arguments:
- snapshots: bfloat16 [128, 256, 8192], P('tm', None, 'space'), may hold values from -6 to 6
- weights: float32 [8192], P('space'), may hold values from 6.1035156e-05 to 0.0009765625
Outputs:
- spectra: float32 [128, 128, 2, 128], P('space', 'tm')
All inputs are finite; a program needn't handle non-finite values.
Results may differ from a plain program's by a relative error of at most 0.0027.
Values may be sent and summed in bfloat16 or wider, within the bound.
A program may use at most 192 MiB of HBM per device.

v0:
```python
import functools
import math

import jax
import jax.numpy as jnp
import numpy as np
from jax import lax
from jax.experimental import pallas as pl
from jax.experimental.pallas import tpu as pltpu
from jax.sharding import PartitionSpec as P

MESH = pl.DeviceIdType.MESH
WIDTH = 128
GROUP = 16


def make_table(length, count):
    steps_t = np.arange(length, dtype=np.int32)
    freqs = np.arange(count, dtype=np.int32)
    turn = np.float32(2.0 * math.pi / length)
    phase = (freqs[:, None] * steps_t[None, :] % length).astype(np.float32) * turn
    hann = np.float32(0.5) - np.float32(0.5) * np.cos(steps_t.astype(np.float32) * turn)
    factor = np.float32(1.0 / math.sqrt(3.0 * length / 8.0))
    table = np.concatenate([np.cos(phase), -np.sin(phase)], axis=0) * hann[None, :] * factor
    return jnp.asarray(table.astype(jnp.bfloat16))


def swap_matrix():
    size = GROUP * GROUP
    source = np.arange(size).reshape(GROUP, GROUP).T.reshape(-1)
    return jnp.asarray(np.eye(size, dtype=np.float32)[source].astype(jnp.bfloat16))


def order_matrix(unit_size, blocks, n_space):
    size = unit_size * 2 * blocks
    rows = blocks // n_space
    source = np.arange(size).reshape(unit_size, 2, n_space, rows).transpose(2, 0, 1, 3).reshape(-1)
    return jnp.asarray(np.eye(size, dtype=np.float32)[source].astype(jnp.bfloat16))


def partner(me, k, count):
    if count & (count - 1):
        return lax.rem(me + k, count)
    other, bit = 0, 1
    while bit < count:
        have = lax.rem(lax.div(me, bit), 2)
        other = other + bit * (1 - have if k & bit else have)
        bit *= 2
    return other


def kernel(
    n_tm, n_space, width, early, unit_size, later,
    x_ref, w_hbm, table_hbm, swap_hbm, order_hbm, out_buf,
    w_ref, table_ref, swap_ref, order_ref,
    x_buf, rows_buf, outgoing, owned, part, arrived,
    const_sem, x_sem, early_send, early_recv, unit_send, unit_recv, sum_send, sum_recv,
):
    me = lax.axis_index("tm")
    seat = lax.axis_index("space")
    blocks, length, points = x_ref.shape
    half = length // 2
    freqs = half // n_tm
    tiles = points // width
    steps = blocks // GROUP * tiles
    units = freqs // unit_size
    total = blocks * n_tm
    rows = total // n_space
    slab = unit_size * 2 * rows
    peers = list(range(n_tm - 1, 0, -1))
    seats = list(range(n_space - 1, 0, -1))

    def place(step):
        start = pl.multiple_of(step // tiles * GROUP, GROUP)
        return start, pl.multiple_of(step % tiles * width, width)

    def load(step):
        start, column = place(step)
        return pltpu.make_async_copy(
            x_ref.at[pl.ds(start, GROUP), :, pl.ds(column, width)],
            x_buf.at[step % 2],
            x_sem.at[step % 2],
        )

    def early_copy(step, k):
        start, column = place(step)
        return pltpu.make_async_remote_copy(
            src_ref=outgoing.at[k - 1, pl.ds(0, early), :, pl.ds(start, GROUP), pl.ds(column, width)],
            dst_ref=owned.at[
                pl.ds(0, early), :, pl.ds(pl.multiple_of(me * blocks + start, GROUP), GROUP), pl.ds(column, width)
            ],
            send_sem=early_send.at[step, k - 1],
            recv_sem=early_recv.at[step, k - 1],
            device_id={"tm": partner(me, k, n_tm)},
            device_id_type=MESH,
        )

    def later_copy(item, k):
        first, size, column, span = later[item]
        columns = pl.ds(column, span)
        return pltpu.make_async_remote_copy(
            src_ref=outgoing.at[k - 1, pl.ds(first, size), :, :, columns],
            dst_ref=owned.at[pl.ds(first, size), :, pl.ds(pl.multiple_of(me * blocks, GROUP), blocks), columns],
            send_sem=unit_send.at[item, k - 1],
            recv_sem=unit_recv.at[item, k - 1],
            device_id={"tm": partner(me, k, n_tm)},
            device_id_type=MESH,
        )

    def sum_copy(unit, k):
        owner = partner(seat, k, n_space)
        return pltpu.make_async_remote_copy(
            src_ref=part.at[unit, owner],
            dst_ref=arrived.at[unit, k - 1],
            send_sem=sum_send.at[unit],
            recv_sem=sum_recv.at[unit],
            device_id={"space": owner},
            device_id_type=MESH,
        )

    constants = [
        pltpu.make_async_copy(pair[0], pair[1], const_sem.at[i])
        for i, pair in enumerate(
            [(table_hbm, table_ref), (w_hbm, w_ref), (swap_hbm, swap_ref), (order_hbm, order_ref)]
        )
    ]
    constants[0].start()
    constants[1].start()
    load(0).start()
    constants[2].start()
    constants[3].start()
    barrier = pltpu.get_barrier_semaphore()
    for k in range(1, n_tm):
        pl.semaphore_signal(barrier, inc=1, device_id={"tm": partner(me, k, n_tm)}, device_id_type=MESH)
    for k in range(1, n_space):
        pl.semaphore_signal(barrier, inc=1, device_id={"space": partner(seat, k, n_space)}, device_id_type=MESH)
    for copy in constants:
        copy.wait()

    def transform(step, carry):
        start, column = place(step)

        @pl.when(step + 1 < steps)
        def _():
            load(step + 1).start()

        load(step).wait()
        scale = jnp.sqrt(w_ref[:, pl.ds(column, width)])

        def one(b, inner):
            product = jnp.dot(table_ref[...], x_buf[step % 2, b], preferred_element_type=jnp.float32)
            rows_buf[b] = (product * scale).astype(jnp.bfloat16)
            return inner

        lax.fori_loop(0, GROUP, one, 0, unroll=2)
        def exchange(k, f):
            target = owned if k == 0 else outgoing.at[k - 1]
            base = partner(me, k, n_tm) * freqs
            offset = me * blocks + start if k == 0 else start
            for c in range(2):
                row = pl.multiple_of(c * half + base + f, GROUP)
                taken = rows_buf[:, pl.ds(row, GROUP), :].reshape(GROUP * GROUP, width)
                swapped = jnp.dot(swap_ref[...], taken, preferred_element_type=jnp.float32)
                target[
                    pl.ds(f, GROUP), c, pl.ds(pl.multiple_of(offset, GROUP), GROUP), pl.ds(column, width)
                ] = swapped.astype(jnp.bfloat16).reshape(GROUP, GROUP, width)

        starts = range(0, freqs, GROUP)
        first = [(k, f) for f in starts if f < early for k in peers]
        rest = [(k, f) for f in starts if f >= early for k in peers] + [(0, f) for f in starts]
        for k, f in first:
            exchange(k, f)

        @pl.when(step == 0)
        def _():
            pl.semaphore_wait(barrier, n_tm + n_space - 2)

        for k in peers:
            early_copy(step, k).start()
        for k, f in rest:
            exchange(k, f)
        return carry

    lax.fori_loop(0, steps, transform, 0)

    for item in range(len(later)):
        for k in peers:
            later_copy(item, k).start()

    def early_wait(step, carry):
        for k in range(1, n_tm):
            early_copy(step, k).wait()
        return carry

    lax.fori_loop(0, steps, early_wait, 0)

    def finish(unit):
        pltpu.make_async_copy(arrived.at[unit], arrived.at[unit], sum_recv.at[unit]).wait()
        value = part[unit, seat].astype(jnp.float32)
        for k in range(n_space - 1):
            value = value + arrived[unit, k].astype(jnp.float32)
        for i in range(2 * unit_size):
            out_buf[:, pl.ds(unit * 2 * unit_size + i, 1), :] = value[i * rows : (i + 1) * rows][:, None, :]

    def cross(unit, carry):
        for item in range(len(later) - 1):

            @pl.when(unit == later[item][0] // unit_size)
            def _(item=item):
                for k in peers:
                    later_copy(item, k).wait_recv()

        pieces = []
        grams = []
        for column in (0, points // 2):
            if column:

                @pl.when(unit == units - 1)
                def _():
                    for k in peers:
                        later_copy(len(later) - 1, k).wait_recv()

            for i in range(unit_size):
                both = owned[unit * unit_size + i, :, :, pl.ds(column, points // 2)]
                both = both.reshape(2 * total, points // 2)
                grams.append(
                    lax.dot_general(both, both, (((1,), (1,)), ((), ())), preferred_element_type=jnp.float32)
                )
        for i in range(unit_size):
            gram = grams[i] + grams[unit_size + i]
            pieces.append(gram[:total, :total] + gram[total:, total:])
            pieces.append(gram[:total, total:] - gram[total:, :total])
        pieces = [piece.astype(jnp.bfloat16) for piece in pieces]
        if rows % GROUP == 0:
            for i, piece in enumerate(pieces):
                for d in range(n_space):
                    part[unit, d, i * rows : (i + 1) * rows, :] = piece[d * rows : (d + 1) * rows]
        else:
            ordered = jnp.dot(
                order_ref[...], jnp.concatenate(pieces, axis=0), preferred_element_type=jnp.float32
            )
            part[unit] = ordered.astype(jnp.bfloat16).reshape(n_space, slab, total)

        @pl.when(unit > 1)
        def _():
            finish(unit - 2)

        for k in seats:
            sum_copy(unit, k).start()

        return carry

    lax.fori_loop(0, units, cross, 0)
    for unit in (units - 2, units - 1):
        finish(unit)

    def sent(unit, carry):
        pltpu.make_async_copy(arrived.at[unit], arrived.at[unit], sum_send.at[unit]).wait()
        return carry

    lax.fori_loop(0, units, sent, 0)
    for item in range(len(later)):
        for k in peers:
            later_copy(item, k).wait_send()


def per_device(n_tm, n_space, snapshots, weights):
    blocks, length, points = snapshots.shape
    total, freqs = blocks * n_tm, length // 2 // n_tm
    rows = total // n_space
    unit_size = max(1, GROUP // (2 * rows))
    units = freqs // unit_size
    slab = unit_size * 2 * rows
    width = min(WIDTH, points)
    early = max(freqs // 4, unit_size)
    later, first = [], early
    while first + unit_size < freqs:
        size = max(unit_size, (freqs - first) // (2 * unit_size) * unit_size)
        later.append((first, size, 0, points))
        first += size
    later += [(first, unit_size, column, points // 2) for column in (0, points // 2)]
    steps = blocks // GROUP * (points // width)
    hbm = pl.BlockSpec(memory_space=pl.ANY)
    bf16 = jnp.bfloat16
    table = make_table(length, length // 2)
    swap = swap_matrix()
    order = swap if rows % GROUP == 0 else order_matrix(unit_size, total, n_space)
    sums = pl.pallas_call(
        functools.partial(kernel, n_tm, n_space, width, early, unit_size, later),
        out_shape=jax.ShapeDtypeStruct((rows, freqs * 2, total), jnp.float32),
        in_specs=[hbm] * 5,
        out_specs=pl.BlockSpec(memory_space=pltpu.VMEM),
        scratch_shapes=[
            pltpu.VMEM((1, points), jnp.float32),
            pltpu.VMEM(table.shape, bf16),
            pltpu.VMEM(swap.shape, bf16),
            pltpu.VMEM(order.shape, bf16),
            pltpu.VMEM((2, GROUP, length, width), bf16),
            pltpu.VMEM((GROUP, length, width), bf16),
            pltpu.VMEM((n_tm - 1, freqs, 2, blocks, points), bf16),
            pltpu.VMEM((freqs, 2, total, points), bf16),
            pltpu.VMEM((units, n_space, slab, total), bf16),
            pltpu.VMEM((units, n_space - 1, slab, total), bf16),
            pltpu.SemaphoreType.DMA((4,)),
            pltpu.SemaphoreType.DMA((2,)),
            pltpu.SemaphoreType.DMA((steps, n_tm - 1)),
            pltpu.SemaphoreType.DMA((steps, n_tm - 1)),
            pltpu.SemaphoreType.DMA((len(later), n_tm - 1)),
            pltpu.SemaphoreType.DMA((len(later), n_tm - 1)),
            pltpu.SemaphoreType.DMA((units,)),
            pltpu.SemaphoreType.DMA((units,)),
        ],
        compiler_params=pltpu.CompilerParams(
            collective_id=0, has_side_effects=True, vmem_limit_bytes=60 * 1024 * 1024
        ),
    )(
        snapshots,
        weights[None, :],
        table,
        swap,
        order,
    )
    return sums.reshape(rows, freqs, 2, total)


def solution(mesh):
    return jax.shard_map(
        functools.partial(per_device, mesh.shape["tm"], mesh.shape["space"]),
        mesh=mesh,
        in_specs=(P("tm", None, "space"), P("space")),
        out_specs=P("space", "tm", None, None),
        check_vma=False,
    )
```

profile of v0, /device:TPU:0, one launch (start us, length us, event | category | flops | bytes accessed | tf_op | source)
XLA Modules:
  0.0 197.6 jit_solution(8600791642271392827)
XLA Ops:
  0.0 195.7 %shard_map.46 = f32[16,64,128]{2,1,0:T(8,128)} custom-call(bf16[32,256,1024]{2,1,0:T(8,128)(2,1)} %x_ref.1, f32[1,1024]{1,0:T(1,128)} %bitcast.3, bf16[256,256]{1,0:T(8,128)(2,1)} %constant.4.clone.table_hbm, bf16[256,256]{1,0:T(8,128)(2,1)} %constant.5.clone.swap_hbm.order_hbm, bf16[256,256]{1,0:T(8,128)(2,1)} %constant.5.clone.swap_hbm.order_hbm), custom_call_target="tpu_custom_call" | custom-call | tf_op jit(solution)/shard_map/pallas_call | solution.py:288
  195.7 1.9 copy.6
where the time goes:
time: 198 us
  Pallas kernels  196 us (99%)
    pallas_call x1, Pallas kernels, per_device(): pl.pallas_call(functools.partial(kernel, n_tm, n_space, width, early, uni...  196 us

commit v1 on v0

--- a/solution.py
+++ b/solution.py
@@ -49,12 +49,17 @@
     return other
 
 
+def signal(sem, where):
+    pl.semaphore_signal(sem, inc=1, device_id=where, device_id_type=MESH)
+
+
 def kernel(
     n_tm, n_space, width, early, unit_size, later,
     x_ref, w_hbm, table_hbm, swap_hbm, order_hbm, out_buf,
     w_ref, table_ref, swap_ref, order_ref,
     x_buf, rows_buf, outgoing, owned, part, arrived,
     const_sem, x_sem, early_send, early_recv, unit_send, unit_recv, sum_send, sum_recv,
+    relay_sem, up_sem, down_sem,
 ):
     me = lax.axis_index("tm")
     seat = lax.axis_index("space")
@@ -68,6 +73,8 @@
     rows = total // n_space
     slab = unit_size * 2 * rows
     peers = list(range(n_tm - 1, 0, -1))
+    near = [k for k in peers if k & (k - 1) == 0]
+    far = [k for k in peers if k & (k - 1)]
     seats = list(range(n_space - 1, 0, -1))
 
     def place(step):
@@ -129,11 +136,21 @@
     load(0).start()
     constants[2].start()
     constants[3].start()
+    bits = [1 << i for i in range(n_tm.bit_length() - 1)]
+    has_left = jnp.where(seat > 0, 1, 0)
+    has_right = jnp.where(seat < n_space - 1, 1, 0)
     barrier = pltpu.get_barrier_semaphore()
-    for k in range(1, n_tm):
-        pl.semaphore_signal(barrier, inc=1, device_id={"tm": partner(me, k, n_tm)}, device_id_type=MESH)
-    for k in range(1, n_space):
-        pl.semaphore_signal(barrier, inc=1, device_id={"space": partner(seat, k, n_space)}, device_id_type=MESH)
+    for k in bits:
+        signal(barrier, {"tm": partner(me, k, n_tm)})
+
+    @pl.when(seat > 0)
+    def _():
+        signal(barrier, {"space": seat - 1})
+
+    @pl.when(seat < n_space - 1)
+    def _():
+        signal(barrier, {"space": seat + 1})
+
     for copy in constants:
         copy.wait()
 
@@ -147,12 +164,12 @@
         load(step).wait()
         scale = jnp.sqrt(w_ref[:, pl.ds(column, width)])
 
-        def one(b, inner):
-            product = jnp.dot(table_ref[...], x_buf[step % 2, b], preferred_element_type=jnp.float32)
-            rows_buf[b] = (product * scale).astype(jnp.bfloat16)
-            return inner
-
-        lax.fori_loop(0, GROUP, one, 0, unroll=2)
+        for b in range(0, GROUP, 2):
+            pair = jnp.concatenate([x_buf[step % 2, b], x_buf[step % 2, b + 1]], axis=1)
+            product = jnp.dot(table_ref[...], pair, preferred_element_type=jnp.float32)
+            rows_buf[b] = (product[:, :width] * scale).astype(jnp.bfloat16)
+            rows_buf[b + 1] = (product[:, width:] * scale).astype(jnp.bfloat16)
+
         def exchange(k, f):
             target = owned if k == 0 else outgoing.at[k - 1]
             base = partner(me, k, n_tm) * freqs
@@ -173,12 +190,24 @@
 
         @pl.when(step == 0)
         def _():
-            pl.semaphore_wait(barrier, n_tm + n_space - 2)
-
-        for k in peers:
+            pl.semaphore_wait(barrier, len(bits) + has_left + has_right)
+            for i, k in enumerate(bits[1:]):
+                signal(relay_sem.at[i], {"tm": partner(me, k, n_tm)})
+
+        for k in near:
             early_copy(step, k).start()
+
         for k, f in rest:
             exchange(k, f)
+
+        @pl.when(step == 0)
+        def _():
+            for i, k in enumerate(bits[1:]):
+                pl.semaphore_wait(relay_sem.at[i], 1)
+
+        for k in far:
+            early_copy(step, k).start()
+
         return carry
 
     lax.fori_loop(0, steps, transform, 0)
@@ -186,6 +215,19 @@
     for item in range(len(later)):
         for k in peers:
             later_copy(item, k).start()
+
+    @pl.when(seat > 0)
+    def _():
+        pl.semaphore_wait(up_sem, 1)
+
+    @pl.when(seat < n_space - 1)
+    def _():
+        signal(up_sem, {"space": seat + 1})
+        pl.semaphore_wait(down_sem, 1)
+
+    @pl.when(seat > 0)
+    def _():
+        signal(down_sem, {"space": seat - 1})
 
     def early_wait(step, carry):
         for k in range(1, n_tm):
@@ -241,12 +283,12 @@
             )
             part[unit] = ordered.astype(jnp.bfloat16).reshape(n_space, slab, total)
 
+        for k in seats:
+            sum_copy(unit, k).start()
+
         @pl.when(unit > 1)
         def _():
             finish(unit - 2)
-
-        for k in seats:
-            sum_copy(unit, k).start()
 
         return carry
 
@@ -309,6 +351,9 @@
             pltpu.SemaphoreType.DMA((len(later), n_tm - 1)),
             pltpu.SemaphoreType.DMA((units,)),
             pltpu.SemaphoreType.DMA((units,)),
+            pltpu.SemaphoreType.REGULAR((max(1, n_tm.bit_length() - 2),)),
+            pltpu.SemaphoreType.REGULAR,
+            pltpu.SemaphoreType.REGULAR,
         ],
         compiler_params=pltpu.CompilerParams(
             collective_id=0, has_side_effects=True, vmem_limit_bytes=60 * 1024 * 1024

time: 198 us -> 197 us (level)
  no operation moved by 1% of the time
where the time goes in v1:
time: 197 us
  Pallas kernels  195 us (99%)
    pallas_call x1, Pallas kernels, per_device(): pl.pallas_call(functools.partial(kernel, n_tm, n_space, width, early, uni...  195 us

profile of v1, /device:TPU:0, one launch (start us, length us, event | category | flops | bytes accessed | tf_op | source)
XLA Modules:
  0.0 196.5 jit_solution(15645240684484230753)
XLA Ops:
  0.0 194.6 %shard_map.46 = f32[16,64,128]{2,1,0:T(8,128)} custom-call(bf16[32,256,1024]{2,1,0:T(8,128)(2,1)} %x_ref.1, f32[1,1024]{1,0:T(1,128)} %bitcast.3, bf16[256,256]{1,0:T(8,128)(2,1)} %constant.4.clone.table_hbm, bf16[256,256]{1,0:T(8,128)(2,1)} %constant.5.clone.swap_hbm.order_hbm, bf16[256,256]{1,0:T(8,128)(2,1)} %constant.5.clone.swap_hbm.order_hbm), custom_call_target="tpu_custom_call" | custom-call | tf_op jit(solution)/shard_map/pallas_call | solution.py:330
  194.6 1.9 copy.6
